TPU v7x, 32 devices: a whole 2x2x4 slice. The times are simulated.
32 devices in a mesh: ia: 4 (over x, core), ja: 8 (over z, y).
Axes of the slice: x: 2, y: 2, z: 4, core: 2. Of those that a mesh axis runs over, the one named last changes fastest.
Arguments:
- star_pos: float32 [3, 32768], P(None, ('ia', 'ja')), may hold values from -6 to 6
- star_vel: float32 [3, 32768], P(None, ('ia', 'ja')), may hold values from -3 to 3
- star_acc: float32 [3, 32768], P(None, ('ia', 'ja')), may hold values from -3 to 3
- star_jerk: float32 [3, 32768], P(None, ('ia', 'ja')), may hold values from -6 to 6
- star_mass: float32 [32768], P(('ia', 'ja')), may hold values from 6.1035157e-06 to 0.00015258789
- star_level: int32 [32768], P(('ia', 'ja')), may hold values from 0 to 5, as said below
- active_index: int32 [256], P(('ia', 'ja')), may hold values from 0 to 1023, as said below
- active_count: int32 [32], P(('ia', 'ja')), may hold values from 1 to 8, as said below
Outputs:
- updated: float32 [12, 256], P(None, ('ia', 'ja'))
Inputs may be any that keep to these rules, and one draw needn't show every extreme that they name: active_count[b] is the number of active stars of owner block b; some block has exactly 8, not always the same one. `active_index`: the slots of owner block b hold distinct local star numbers of that block; the first active_count[b] of them are exactly the stars of the block with star_level 3 or more, the others name inactive stars of the block. `star_level`: A star is active at this step exactly when its level is 3 or more.
All inputs are finite; a program needn't handle non-finite values.
Results may differ from a plain program's by a relative error of at most 0.0003.
Values sent between devices are 32-bit elements; how exact they have to be, the bound alone decides.
A program may use at most 64 MiB of HBM per device.

v0:
```python
import math

import jax
import jax.numpy as jnp
from jax import lax
from jax.sharding import PartitionSpec as P

tick_now = 44
top_level = 5
tick_length = 0.125
soft_square = 0.0001


def star_age(levels):
    periods = jnp.left_shift(jnp.ones_like(levels), top_level - levels)
    remains = jnp.remainder(jnp.full_like(levels, tick_now), periods)
    ticks = jnp.where(remains == 0, periods, remains)
    return ticks.astype(jnp.float32) * tick_length


def predict(positions, velocity, accelerations, jerk_rates, star_ages):
    elapsed = star_ages[None, :]
    new_pos = positions + elapsed * (
        velocity + elapsed * (accelerations * 0.5 + elapsed * jerk_rates / 6.0)
    )
    new_vel = velocity + elapsed * (accelerations + elapsed * jerk_rates * 0.5)
    return (new_pos, new_vel)


def pair_block(targets, sources):
    delta_pos = [sources[axis_num][None, :] - targets[axis_num][:, None] for axis_num in range(3)]
    delta_vel = [
        sources[3 + axis_num][None, :] - targets[3 + axis_num][:, None] for axis_num in range(3)
    ]
    squared = (
        delta_pos[0] * delta_pos[0]
        + delta_pos[1] * delta_pos[1]
        + delta_pos[2] * delta_pos[2]
        + soft_square
    )
    inverse = lax.rsqrt(squared)
    inverse_sq = inverse * inverse
    strength = sources[6][None, :] * inverse * inverse_sq
    radial = (
        3.0
        * (delta_pos[0] * delta_vel[0] + delta_pos[1] * delta_vel[1] + delta_pos[2] * delta_vel[2])
        * inverse_sq
    )
    results = [jnp.sum(strength * delta_pos[axis_num], axis=1) for axis_num in range(3)]
    results = results + [
        jnp.sum(strength * (delta_vel[axis_num] - radial * delta_pos[axis_num]), axis=1)
        for axis_num in range(3)
    ]
    return jnp.stack(results)


def correct(targets, forces, old_acc, old_jerk, step_sizes, live_mask):
    new_acc = forces[:3]
    new_jerk = forces[3:]
    elapsed = step_sizes[None, :]
    change = old_acc - new_acc
    snap_part = -6.0 * change - elapsed * (4.0 * old_jerk + 2.0 * new_jerk)
    crackle_part = 12.0 * change + 6.0 * elapsed * (old_jerk + new_jerk)
    cor_pos = targets[:3] + elapsed * elapsed * (snap_part / 24.0 + crackle_part / 120.0)
    cor_vel = targets[3:] + elapsed * (snap_part / 6.0 + crackle_part / 24.0)
    stacked = jnp.concatenate([cor_pos, cor_vel, new_acc, new_jerk], 0)
    return jnp.where(live_mask[None, :], stacked, 0.0)


def tile_forces(targets, sources):
    slot_count = targets.shape[1]
    source_count = sources.shape[1]
    tile_rows = math.gcd(slot_count, max(32, slot_count // 16))
    tile_cols = math.gcd(source_count, max(128, 131072 // tile_rows))
    tile_count = slot_count // tile_rows
    col_turns = source_count // tile_cols
    tiles = jnp.transpose(targets.reshape(6, tile_count, tile_rows), (1, 0, 2))
    offsets = jnp.arange(tile_count, dtype=jnp.int32) * tile_rows
    zero_tile = jnp.zeros((6, tile_rows), jnp.float32)

    def compute(target_tile):

        def advance(turn_index, running):
            source_part = lax.dynamic_slice_in_dim(sources, turn_index * tile_cols, tile_cols, 1)
            return running + pair_block(target_tile, source_part)

        return lax.fori_loop(0, col_turns, advance, zero_tile)

    def one_tile(tile_entry):
        target_tile, offset = tile_entry
        return compute(target_tile)

    results = lax.map(one_tile, (tiles, offsets))
    return jnp.transpose(results, (1, 0, 2)).reshape(6, slot_count)


def arrange(targets):
    return (targets, None, None)


def on_device(
    star_pos, star_vel, star_acc, star_jerk, star_mass, star_level, active_index, active_count
):
    capacity = active_index.shape[0]
    star_ages = star_age(star_level)
    pred_pos, pred_vel = predict(star_pos, star_vel, star_acc, star_jerk, star_ages)
    sources = jnp.concatenate([pred_pos, pred_vel, star_mass[None, :]], 0)
    own_targets = jnp.concatenate(
        [jnp.take(pred_pos, active_index, axis=1), jnp.take(pred_vel, active_index, axis=1)], 0
    )
    count_value = active_count.astype(jnp.float32)
    targets, counts = (
        lax.all_gather(own_targets, "ia", axis=1, tiled=True),
        lax.all_gather(count_value, "ia", axis=0, tiled=True),
    )
    prepared, live_total, places = arrange(targets)
    pair_sums = tile_forces(prepared, lax.all_gather(sources, "ja", axis=1, tiled=True))
    forces = lax.psum_scatter(pair_sums, "ia", scatter_dimension=1, tiled=True)
    live_mask = jnp.arange(capacity, dtype=jnp.int32) < active_count[0]
    old_acc = jnp.take(star_acc, active_index, axis=1)
    old_jerk = jnp.take(star_jerk, active_index, axis=1)
    step_sizes = jnp.take(star_ages, active_index)
    return correct(own_targets, forces, old_acc, old_jerk, step_sizes, live_mask)


def solution(mesh):
    placed = (
        P(None, ("ia", "ja")),
        P(None, ("ia", "ja")),
        P(None, ("ia", "ja")),
        P(None, ("ia", "ja")),
        P(("ia", "ja")),
        P(("ia", "ja")),
        P(("ia", "ja")),
        P(("ia", "ja")),
    )
    return jax.shard_map(
        on_device, mesh=mesh, in_specs=placed, out_specs=P(None, ("ia", "ja")), check_vma=False
    )
```

profile of v0, /device:TPU:0, one launch (start us, length us, event | category | flops | bytes accessed | tf_op | source)
XLA Modules:
  0.0 60.1 jit_solution(17922956348764657168)
XLA Ops:
  0.0 0.0 copy-start.5
  0.0 0.7 %compare_select_fusion.2 = s32[8]{0:T(128)S(1)} fusion(s32[8]{0:T(128)} %param.18), kind=kLoop, calls=%fused_computation.75 | loop fusion | flops 24 | bytes 64 | tf_op jit(solution)/shard_map/jit(_take)/jit(_where)/select_n | solution.py:109
  0.7 0.0 copy-done.5
  0.7 0.1 fusion.18
  0.8 0.0 copy-start.6
  0.8 0.0 copy-start
  0.8 0.0 copy-start.1
  0.9 0.0 copy-start.2
  0.9 0.0 copy-start.3
  0.9 0.6 %gather_fusion = f32[8]{0:T(128)S(1)} fusion(f32[1024]{0:T(1024)S(1)} %fusion.18, s32[1024]{0:T(1024)S(1)} %pad_clamp_fusion), kind=kCustom, calls=%fused_computation.4 | custom fusion | bytes 96 | tf_op jit(solution)/shard_map/jit(_take)/gather | solution.py:122
  1.5 0.0 copy-done.6
  1.5 0.0 copy-done
  1.6 0.0 copy-done.1
  1.6 0.0 copy-done.2
  1.6 0.0 copy-done.3
  1.6 0.2 copy.76
  1.9 0.6 gather_fusion.1
  2.4 0.2 copy.78
  2.6 0.6 gather_fusion.3
  3.2 0.1 select_bitcast_fusion.1
  3.3 0.1 pad_maximum_fusion.1
  3.4 6.2 %all_gather.7 = f32[6,32]{0,1:T(8,128)S(1)} all-gather(f32[6,8]{0,1:T(8,128)S(1)} %pad_maximum_fusion.1), channel_id=1, replica_groups=mesh['ia'=4,'ja'=8] {'ia'}, dimensions={1}, use_global_device_ids=true | all-gather | bytes 960 | tf_op jit(solution)/shard_map/all_gather | solution.py:113
  9.6 0.0 copy-start.4
  9.6 0.1 copy.79
  9.7 0.6 %copy-done.4 = f32[1024]{0:T(1024)S(1)} copy-done((f32[1024]{0:T(1024)S(1)}, f32[1024]{0:T(1024)}, u32[]{:S(2)}) %copy-start.4) | copy-done | bytes 4120
  10.3 31.6 %all_gather.6 = f32[7,8192]{1,0:T(8,128)S(1)} all-gather(f32[7,1024]{1,0:T(8,128)S(1)} %pad_maximum_fusion), channel_id=1, replica_groups=mesh['ia'=4,'ja'=8] {'ja'}, dimensions={1}, use_global_device_ids=true | all-gather | bytes 258048 | tf_op jit(solution)/shard_map/all_gather | solution.py:117
  41.9 3.0 %while.21 = (s32[]{:T(128)}, f32[6,32]{1,0:T(8,128)S(1)}, f32[7,8192]{1,0:T(8,128)S(1)}, f32[6,32]{1,0:T(8,128)S(1)}, s32[]{:T(128)}, /*index=5*/s32[]{:T(128)},...) while((s32[]{:T(128)}, f32[6,32]{1,0:T(8,128)S(1)}, ...), condition=%wide.region_7.9_spmd.clone, body=%wide.region_0.8_spmd.clone.sunk | while | flops 5243085 | bytes 351265 | solution.py:87
  41.9 0.3 fusion.33
  42.2 1.1 %fusion.34 = (f32[32]{0:T(128)S(1)}, f32[32]{0:T(128)S(1)}, f32[32]{0:T(128)S(1)}, f32[32]{0:T(128)S(1)}, f32[32]{0:T(128)S(1)}, /*index=5*/f32[32]{0:T(128)S(1)}) fusion(f32[32]{0:T(128)S(1)} %get-tuple-element.220, f32[4096]{0:T(1024)S(1)} %bitcast.90, f32[32]{0:T(128)S(1)} %get-tuple-element.222, f32[4096]{0:T(1024)S(1)} %bitcast.86, ...), kind=kLoop, calls=%fused_computation.25.clone.1 | loop fusion | flops 5242688 | bytes 116224 | tf_op jit(solution)/shard_map/while/body/eval_jaxpr/while/body/eval_jaxpr/reduce_sum | solution.py:51
  43.4 0.3 fusion.33
  43.7 1.1 %fusion.34 = (f32[32]{0:T(128)S(1)}, f32[32]{0:T(128)S(1)}, f32[32]{0:T(128)S(1)}, f32[32]{0:T(128)S(1)}, f32[32]{0:T(128)S(1)}, /*index=5*/f32[32]{0:T(128)S(1)}) fusion(f32[32]{0:T(128)S(1)} %get-tuple-element.220, f32[4096]{0:T(1024)S(1)} %bitcast.90, f32[32]{0:T(128)S(1)} %get-tuple-element.222, f32[4096]{0:T(1024)S(1)} %bitcast.86, ...), kind=kLoop, calls=%fused_computation.25.clone.1 | loop fusion | flops 5242688 | bytes 116224 | tf_op jit(solution)/shard_map/while/body/eval_jaxpr/while/body/eval_jaxpr/reduce_sum | solution.py:51
  44.9 0.1 copy.80
  45.0 10.1 %all-reduce = f32[6,32]{0,1:T(8,128)S(1)} all-reduce(f32[6,32]{0,1:T(8,128)S(1)} %copy.80), channel_id=2, replica_groups=mesh['ia'=4,'ja'=8] {'ia'}, use_global_device_ids=true, to_apply=%region_8.10.clone | all-reduce | flops 192 | bytes 1536
  55.1 0.0 copy-start.7
  55.1 0.7 %copy-done.7 = u32[32]{0:T(128)S(1)} copy-done((u32[32]{0:T(128)S(1)}, u32[32]{0:T(128)}, u32[]{:S(2)}) %copy-start.7) | copy-done | bytes 152
  55.8 0.6 dynamic-slice.1
  57.0 0.2 copy.77
  57.3 0.6 gather_fusion.2
  57.8 0.2 copy.81
  58.1 0.6 gather_fusion.4
  58.6 0.1 multiply_add_fusion.3
  58.7 0.1 multiply_add_fusion.2
  59.4 0.7 %maximum_select_fusion = f32[12,8]{0,1:T(8,128)} fusion(f32[6,8]{0,1:T(8,128)S(1)} %constant_dynamic-slice_fusion.1, f32[3,8]{0,1:T(8,128)S(1)} %multiply_add_fusion.2, f32[3,8]{0,1:T(8,128)S(1)} %get-tuple-element.153, pred[8]{0:T(512)(128)(4,1)S(1)} %iota_compare_fusion), kind=kLoop, calls=%fused_computation.58 | loop fusion | flops 288 | bytes 776 | tf_op jit(solution)/shard_map/jit(_where)/select_n | solution.py:67
  (14 shorter events, 0.1 us)
Async XLA Ops:
  0.0 0.7 %copy-start.5 = (s32[1024]{0:T(1024)S(1)}, s32[1024]{0:T(1024)}, u32[]{:S(2)}) copy-start(s32[1024]{0:T(1024)} %param.17) | copy-start | bytes 12292
  0.8 0.7 %copy-start.6 = (s32[8]{0:T(128)S(1)}, s32[8]{0:T(128)}, u32[]{:S(2)}) copy-start(s32[8]{0:T(128)} %param.18) | copy-start | bytes 100
  0.8 0.7 %copy-start = (f32[3,1024]{1,0:T(4,128)S(1)}, f32[3,1024]{1,0:T(4,128)}, u32[]{:S(2)}) copy-start(f32[3,1024]{1,0:T(4,128)} %param.14) | copy-start | bytes 36868
  0.8 0.7 %copy-start.1 = (f32[3,1024]{1,0:T(4,128)S(1)}, f32[3,1024]{1,0:T(4,128)}, u32[]{:S(2)}) copy-start(f32[3,1024]{1,0:T(4,128)} %param.15) | copy-start | bytes 36868
  0.9 0.7 %copy-start.2 = (f32[3,1024]{1,0:T(4,128)S(1)}, f32[3,1024]{1,0:T(4,128)}, u32[]{:S(2)}) copy-start(f32[3,1024]{1,0:T(4,128)} %param.12) | copy-start | bytes 36868
  0.9 0.7 %copy-start.3 = (f32[3,1024]{1,0:T(4,128)S(1)}, f32[3,1024]{1,0:T(4,128)}, u32[]{:S(2)}) copy-start(f32[3,1024]{1,0:T(4,128)} %param.13) | copy-start | bytes 36868
  9.6 0.7 %copy-start.4 = (f32[1024]{0:T(1024)S(1)}, f32[1024]{0:T(1024)}, u32[]{:S(2)}) copy-start(f32[1024]{0:T(1024)} %param.16) | copy-start | bytes 12292
  55.1 0.7 %copy-start.7 = (u32[32]{0:T(128)S(1)}, u32[32]{0:T(128)}, u32[]{:S(2)}) copy-start(u32[32]{0:T(128)} %constant.128) | copy-start | bytes 388
where the time goes:
time: 60.5 us; the launch traced here: 60.1 us
  blocking collectives  48 us (79%)
  local copies, waits for them, and re-layouts  6.49 us (11%)
  other arithmetic  4.14 us (7%)
  between operations  1.45 us (2%)
    all_gather x1, blocking collectives, on_device(): lax.all_gather(sources, 'ja', axis=1, tiled=True)  31.6 us
    unnamed x1, blocking collectives  10.1 us
    all_gather x1, blocking collectives, on_device(): lax.all_gather(own_targets, 'ia', axis=1, tiled=True)  6.23 us
    unnamed x21, local copies, waits for them, and re-layouts  2.47 us
    reduce_sum x2, other arithmetic, pair_block(): jnp.sum(strength * (delta_vel[axis_num] - radial * delta_pos[axis_num]),...  2.3 us

commit v1 on v0

v1 whole, which is shorter than its diff:
```python
import functools

import jax
import jax.numpy as jnp
from jax import lax
from jax.experimental import pallas as pl
from jax.experimental.pallas import tpu as pltpu
from jax.sharding import PartitionSpec as P

tick_now = 44
top_level = 5
tick_length = 0.125
soft_square = 0.0001

LANES = 128
SOURCE_PARTS = 2


def kernel(
    shape, pos_hbm, vel_hbm, acc_hbm, jerk_hbm, mass_hbm, level_hbm, idx_hbm, cnt_hbm, out_ref,
    pos, vel, acc, jerk, mass, level, idx, cnt, src, tgt, sums, part, got,
    in_sem, src_send, src_recv, tgt_send, tgt_recv, red_send, red_recv,
):
    n_ia, n_ja, s = shape
    n_lo = n_ja // s
    t = n_ia * n_lo
    stars = pos.shape[1]
    cap = idx.shape[0]
    ia, ja = lax.axis_index("ia"), lax.axis_index("ja")
    hi, lo = ja // n_lo, ja % n_lo
    me = ia * n_lo + lo

    def t_device(k):
        other = (me + k) % t
        return (other // n_lo, hi * n_lo + other % n_lo)

    def s_device(j):
        return (ia, ((hi + j) % s) * n_lo + lo)

    def src_copy(j):
        return pltpu.make_async_remote_copy(
            src_ref=src.at[0], dst_ref=src.at[j], send_sem=src_send.at[j],
            recv_sem=src_recv.at[j], device_id=s_device(j),
            device_id_type=pl.DeviceIdType.MESH)

    def tgt_copy(k):
        return pltpu.make_async_remote_copy(
            src_ref=tgt.at[0], dst_ref=tgt.at[k], send_sem=tgt_send.at[k],
            recv_sem=tgt_recv.at[k], device_id=t_device(k),
            device_id_type=pl.DeviceIdType.MESH)

    def red_copy(k):
        return pltpu.make_async_remote_copy(
            src_ref=part.at[k], dst_ref=got.at[k], send_sem=red_send.at[k],
            recv_sem=red_recv.at[k], device_id=t_device(t - k),
            device_id_type=pl.DeviceIdType.MESH)

    def each(low, high, body):
        def step(k, carry):
            body(k)
            return carry
        lax.fori_loop(low, high, step, 0)

    barrier = pltpu.get_barrier_semaphore()

    def greet(device):
        pl.semaphore_signal(barrier, inc=1, device_id=device,
                            device_id_type=pl.DeviceIdType.MESH)

    loads = [
        pltpu.make_async_copy(a, b, in_sem.at[i])
        for i, (a, b) in enumerate(
            [(level_hbm, level), (pos_hbm, pos), (vel_hbm, vel), (acc_hbm, acc),
             (jerk_hbm, jerk), (mass_hbm, mass), (idx_hbm, idx), (cnt_hbm, cnt)])
    ]
    for load in loads:
        load.start()
    each(1, t, lambda k: greet(t_device(k)))
    each(1, s, lambda j: greet(s_device(j)))
    for load in loads:
        load.wait()

    periods = jnp.left_shift(jnp.ones((1, stars), jnp.int32), top_level - level[...])
    remains = jnp.bitwise_and(tick_now, periods - 1)
    age = jnp.where(remains == 0, periods, remains).astype(jnp.float32) * tick_length
    pred_pos = pos[...] + age * (
        vel[...] + age * (acc[...] * 0.5 + age * jerk[...] * (1.0 / 6.0)))
    pred_vel = vel[...] + age * (acc[...] + age * jerk[...] * 0.5)
    src[0, 0:3] = pred_pos
    src[0, 3:6] = pred_vel
    src[0, 6:7] = mass[...]
    src[0, 7:8] = age

    pl.semaphore_wait(barrier, t + s - 2)
    each(1, s, lambda j: src_copy(j).start())

    slot = lax.broadcasted_iota(jnp.int32, (cap, stars), 0)
    want = jnp.zeros((cap, stars), jnp.int32)
    for i in range(cap):
        want = jnp.where(slot == i, idx[i], want)
    mask = lax.broadcasted_iota(jnp.int32, (cap, stars), 1) == want

    def pick(row):
        return jnp.sum(jnp.where(mask, row, 0.0), axis=1, keepdims=True)

    lane = lax.broadcasted_iota(jnp.int32, (cap, LANES), 1)

    def columns(values):
        tile = jnp.zeros((cap, LANES), jnp.float32)
        for i, value in enumerate(values):
            tile = jnp.where(lane == i, value, tile)
        return tile

    own = [pick(src[0, q:q + 1]) for q in range(6)]
    tgt[0] = columns(own)
    each(1, t, lambda k: tgt_copy(k).start())

    def pairs(k, j, totals):
        tile = tgt[k]
        target = [jnp.broadcast_to(tile[:, q:q + 1], (cap, LANES)) for q in range(6)]
        totals = list(totals)
        for c in range(stars // LANES):
            row = [src[j, q:q + 1, c * LANES:(c + 1) * LANES] for q in range(7)]
            d = [row[q] - target[q] for q in range(3)]
            w = [row[3 + q] - target[3 + q] for q in range(3)]
            u = lax.rsqrt(d[0] * d[0] + d[1] * d[1] + d[2] * d[2] + soft_square)
            u2 = u * u
            m = row[6] * u * u2
            r = 3.0 * (d[0] * w[0] + d[1] * w[1] + d[2] * w[2]) * u2
            for q in range(3):
                totals[q] = totals[q] + m * d[q]
                totals[3 + q] = totals[3 + q] + m * (w[q] - r * d[q])
        return totals

    zeros = [jnp.zeros((cap, LANES), jnp.float32)] * 6

    def near(k):
        totals = pairs(k, 0, zeros)
        for q in range(6):
            sums[k, q] = totals[q]

    def far(k, j_low):
        totals = [sums[k, q] for q in range(6)]
        totals = lax.fori_loop(
            j_low, s, lambda j, carry: tuple(pairs(k, j, carry)), tuple(totals))
        part[k] = columns([jnp.sum(x, axis=1, keepdims=True) for x in totals])

    near(0)
    old = [pick(acc[q:q + 1, :]) for q in range(3)] + [pick(jerk[q:q + 1, :]) for q in range(3)]
    h = pick(src[0, 7:8])

    def near_step(k):
        tgt_copy(k).wait_recv()
        near(k)

    each(1, t, near_step)
    each(1, s, lambda j: src_copy(j).wait_recv())

    def far_step(k):
        far(k, 1)
        red_copy(k).start()

    each(1, t, far_step)
    far(0, 1)

    def collect(k, total):
        red_copy(k).wait_recv()
        return total + got[k]

    total = lax.fori_loop(1, t, collect, part[0])
    force = [total[:, q:q + 1] for q in range(6)]
    rows = [None] * 12
    for q in range(3):
        new_acc, new_jerk = force[q], force[3 + q]
        change = old[q] - new_acc
        snap = -6.0 * change - h * (4.0 * old[3 + q] + 2.0 * new_jerk)
        crackle = 12.0 * change + 6.0 * h * (old[3 + q] + new_jerk)
        rows[q] = own[q] + h * h * (snap * (1.0 / 24.0) + crackle * (1.0 / 120.0))
        rows[3 + q] = own[3 + q] + h * (snap * (1.0 / 6.0) + crackle * (1.0 / 24.0))
        rows[6 + q] = new_acc
        rows[9 + q] = new_jerk
    live = lax.broadcasted_iota(jnp.int32, (cap, LANES), 0) < cnt[0]
    result = jnp.where(live, columns(rows), 0.0)
    out_ref[...] = result[:, :12]

    def drain(k):
        tgt_copy(k).wait_send()
        red_copy(k).wait_send()

    each(1, t, drain)
    each(1, s, lambda j: src_copy(j).wait_send())


def on_device(shape, star_pos, star_vel, star_acc, star_jerk, star_mass, star_level,
              active_index, active_count):
    n_ia, n_ja, s = shape
    t = n_ia * (n_ja // s)
    stars = star_mass.shape[0]
    cap = active_index.shape[0]
    f32 = jnp.float32
    return pl.pallas_call(
        functools.partial(kernel, shape),
        out_shape=jax.ShapeDtypeStruct((cap, 12), f32),
        in_specs=[pl.BlockSpec(memory_space=pltpu.HBM)] * 8,
        out_specs=pl.BlockSpec(memory_space=pltpu.VMEM),
        scratch_shapes=[
            pltpu.VMEM((3, stars), f32), pltpu.VMEM((3, stars), f32),
            pltpu.VMEM((3, stars), f32), pltpu.VMEM((3, stars), f32),
            pltpu.VMEM((1, stars), f32), pltpu.VMEM((1, stars), jnp.int32),
            pltpu.SMEM((cap,), jnp.int32), pltpu.SMEM((1,), jnp.int32),
            pltpu.VMEM((s, 8, stars), f32),
            pltpu.VMEM((t, cap, LANES), f32),
            pltpu.VMEM((t, 6, cap, LANES), f32),
            pltpu.VMEM((t, cap, LANES), f32),
            pltpu.VMEM((t, cap, LANES), f32),
            pltpu.SemaphoreType.DMA((8,)),
            pltpu.SemaphoreType.DMA((s,)), pltpu.SemaphoreType.DMA((s,)),
            pltpu.SemaphoreType.DMA((t,)), pltpu.SemaphoreType.DMA((t,)),
            pltpu.SemaphoreType.DMA((t,)), pltpu.SemaphoreType.DMA((t,)),
        ],
        compiler_params=pltpu.CompilerParams(collective_id=0, has_side_effects=True),
    )(star_pos, star_vel, star_acc, star_jerk, star_mass.reshape(1, stars),
      star_level.reshape(1, stars), active_index, active_count).T


def solution(mesh):
    n_ia, n_ja = mesh.shape["ia"], mesh.shape["ja"]
    s = SOURCE_PARTS if n_ja % SOURCE_PARTS == 0 else 1
    columns = P(None, ("ia", "ja"))
    flat = P(("ia", "ja"))
    return jax.shard_map(
        functools.partial(on_device, (n_ia, n_ja, s)), mesh=mesh,
        in_specs=(columns,) * 4 + (flat,) * 4, out_specs=columns, check_vma=False)
```

time: 60.5 us -> 19.4 us (0.32)
  blocking collectives: 48 us -> 0 us
  Pallas kernels: 0 us -> 17.3 us
  local copies, waits for them, and re-layouts: 6.49 us -> 1.28 us
  other arithmetic: 4.14 us -> 0 us
  between operations: 1.45 us -> 0.66 us
    all_gather x2 -> x0, blocking collectives: 37.9 us -> none  [the longest x1 31.6 us: on_device(): lax.all_gather(sources, 'ja', axis=1, tiled=True)]
    pallas_call x0 -> x1, Pallas kernels: none -> 17.3 us  [on_device(): pl.pallas_call(functools.partial(kernel, shape), out_shape=jax.ShapeDtype...]
    unnamed x1 -> x0, blocking collectives: 10.1 us -> none
    gather x5 -> x0, local copies, waits for them, and re-layouts: 2.87 us -> none  [the longest x1 0.63 us: on_device(): step_sizes = jnp.take(star_ages, active_index)]
    reduce_sum x2 -> x0, other arithmetic: 2.3 us -> none  [pair_block(): jnp.sum(strength * (delta_vel[axis_num] - radial * delta_pos[axis_num]),...]
    select_n x3 -> x0, other arithmetic: 1.41 us -> none  [the longest x2 0.74 us: on_device(): jnp.take(pred_pos, active_index, axis=1)]
    unnamed x21 -> x1, local copies, waits for them, and re-layouts: 2.47 us -> 1.28 us
where the time goes in v1:
time: 19.4 us; the launch traced here: 19.2 us
  Pallas kernels  17.3 us (89%)
  local copies, waits for them, and re-layouts  1.28 us (7%)
  between operations  0.66 us (3%)
    pallas_call x1, Pallas kernels, on_device(): pl.pallas_call(functools.partial(kernel, shape), out_shape=jax.ShapeDtype...  17.3 us
    unnamed x1, local copies, waits for them, and re-layouts  1.28 us

profile of v1, /device:TPU:0, one launch (start us, length us, event | category | flops | bytes accessed | tf_op | source)
XLA Modules:
  0.0 19.2 jit_solution(9821831769945433123)
XLA Ops:
  0.7 17.3 %shard_map.82 = f32[8,12]{1,0:T(8,128)} custom-call(f32[3,1024]{1,0:T(4,128)} %pos_hbm.1, f32[3,1024]{1,0:T(4,128)} %vel_hbm.1, f32[3,1024]{1,0:T(4,128)} %acc_hbm.1, f32[3,1024]{1,0:T(4,128)} %jerk_hbm.1, f32[1,1024]{1,0:T(1,128)} %bitcast.4, s32[1,1024]{1,0:T(1,128)} %bitcast.5, s32[8]{0:T(128)} %idx_hbm.1, s32[1]{0:T(128)S(6)} %copy.10.cnt_hbm), custom_call_target="tpu_custom_call" | custom-call | tf_op jit(solution)/shard_map/pallas_call | solution.py:201
  17.9 1.3 %copy.11 = f32[12,8]{0,1:T(8,128)} copy(f32[12,8]{0,1:T(8,128)} %bitcast.3) | data formatting | bytes 768

commit v2 on v1

--- a/solution.py
+++ b/solution.py
@@ -13,13 +13,14 @@
 soft_square = 0.0001
 
 LANES = 128
-SOURCE_PARTS = 2
+SOURCE_PARTS = 4
+NEAR = 2
 
 
 def kernel(
     shape, pos_hbm, vel_hbm, acc_hbm, jerk_hbm, mass_hbm, level_hbm, idx_hbm, cnt_hbm, out_ref,
     pos, vel, acc, jerk, mass, level, idx, cnt, src, tgt, sums, part, got,
-    in_sem, src_send, src_recv, tgt_send, tgt_recv, red_send, red_recv,
+    in_sem, src_send, src_recv, tgt_send, tgt_recv, red_send, red_recv, ready,
 ):
     n_ia, n_ja, s = shape
     n_lo = n_ja // s
@@ -28,19 +29,28 @@
     cap = idx.shape[0]
     ia, ja = lax.axis_index("ia"), lax.axis_index("ja")
     hi, lo = ja // n_lo, ja % n_lo
-    me = ia * n_lo + lo
-
-    def t_device(k):
-        other = (me + k) % t
-        return (other // n_lo, hi * n_lo + other % n_lo)
-
-    def s_device(j):
-        return (ia, ((hi + j) % s) * n_lo + lo)
-
-    def src_copy(j):
-        return pltpu.make_async_remote_copy(
-            src_ref=src.at[0], dst_ref=src.at[j], send_sem=src_send.at[j],
-            recv_sem=src_recv.at[j], device_id=s_device(j),
+
+    def t_device(k, sign=1):
+        a, b = k // n_lo, k % n_lo
+        return ((ia + sign * a + n_ia) % n_ia, hi * n_lo + (lo + sign * b + n_lo) % n_lo)
+
+    def nearest(o):
+        up = o + jnp.where(o >= hi, 1, 0)
+        down = s - 1 - o - jnp.where(o >= s - 1 - hi, 1, 0)
+        return jnp.where(2 * hi < s, up, down)
+
+    def src_copy(o):
+        place = nearest(o)
+        return pltpu.make_async_remote_copy(
+            src_ref=src.at[hi], dst_ref=src.at[hi], send_sem=src_send.at[place],
+            recv_sem=src_recv.at[hi], device_id=(ia, place * n_lo + lo),
+            device_id_type=pl.DeviceIdType.MESH)
+
+    def src_arrival(o):
+        place = nearest(o)
+        return pltpu.make_async_remote_copy(
+            src_ref=src.at[place], dst_ref=src.at[place], send_sem=src_send.at[place],
+            recv_sem=src_recv.at[place], device_id=(ia, place * n_lo + lo),
             device_id_type=pl.DeviceIdType.MESH)
 
     def tgt_copy(k):
@@ -52,7 +62,7 @@
     def red_copy(k):
         return pltpu.make_async_remote_copy(
             src_ref=part.at[k], dst_ref=got.at[k], send_sem=red_send.at[k],
-            recv_sem=red_recv.at[k], device_id=t_device(t - k),
+            recv_sem=red_recv.at[k], device_id=t_device(k, -1),
             device_id_type=pl.DeviceIdType.MESH)
 
     def each(low, high, body):
@@ -76,7 +86,8 @@
     for load in loads:
         load.start()
     each(1, t, lambda k: greet(t_device(k)))
-    each(1, s, lambda j: greet(s_device(j)))
+    near_count = jnp.minimum(hi, NEAR) + jnp.minimum(s - 1 - hi, NEAR)
+    each(0, near_count, lambda o: greet((ia, nearest(o) * n_lo + lo)))
     for load in loads:
         load.wait()
 
@@ -86,13 +97,10 @@
     pred_pos = pos[...] + age * (
         vel[...] + age * (acc[...] * 0.5 + age * jerk[...] * (1.0 / 6.0)))
     pred_vel = vel[...] + age * (acc[...] + age * jerk[...] * 0.5)
-    src[0, 0:3] = pred_pos
-    src[0, 3:6] = pred_vel
-    src[0, 6:7] = mass[...]
-    src[0, 7:8] = age
-
-    pl.semaphore_wait(barrier, t + s - 2)
-    each(1, s, lambda j: src_copy(j).start())
+    src[hi, 0:3] = pred_pos
+    src[hi, 3:6] = pred_vel
+    src[hi, 6:7] = mass[...]
+    src[hi, 7:8] = age
 
     slot = lax.broadcasted_iota(jnp.int32, (cap, stars), 0)
     want = jnp.zeros((cap, stars), jnp.int32)
@@ -111,9 +119,22 @@
             tile = jnp.where(lane == i, value, tile)
         return tile
 
-    own = [pick(src[0, q:q + 1]) for q in range(6)]
+    own = [pick(src[hi, q:q + 1]) for q in range(6)]
     tgt[0] = columns(own)
+
+    pl.semaphore_wait(barrier, t - 1 + near_count)
+    if s == 4:
+        @pl.when((hi == 1) | (hi == 2))
+        def clear():
+            pl.semaphore_signal(ready, inc=1, device_id=(ia, (hi - 1) * 3 * n_lo + lo),
+                                device_id_type=pl.DeviceIdType.MESH)
+    each(0, near_count, lambda o: src_copy(o).start())
     each(1, t, lambda k: tgt_copy(k).start())
+    if s == 4:
+        @pl.when((hi == 0) | (hi == 3))
+        def far_pair():
+            pl.semaphore_wait(ready, 1)
+            src_copy(2).start()
 
     def pairs(k, j, totals):
         tile = tgt[k]
@@ -134,34 +155,39 @@
 
     zeros = [jnp.zeros((cap, LANES), jnp.float32)] * 6
 
-    def near(k):
-        totals = pairs(k, 0, zeros)
-        for q in range(6):
-            sums[k, q] = totals[q]
-
-    def far(k, j_low):
-        totals = [sums[k, q] for q in range(6)]
-        totals = lax.fori_loop(
-            j_low, s, lambda j, carry: tuple(pairs(k, j, carry)), tuple(totals))
-        part[k] = columns([jnp.sum(x, axis=1, keepdims=True) for x in totals])
-
-    near(0)
+    def add(k, place, totals, last):
+        totals = pairs(k, place, totals)
+        if last:
+            part[k] = columns([jnp.sum(x, axis=1, keepdims=True) for x in totals])
+        else:
+            for q in range(6):
+                sums[k, q] = totals[q]
+
+    add(0, hi, zeros, s == 1)
     old = [pick(acc[q:q + 1, :]) for q in range(3)] + [pick(jerk[q:q + 1, :]) for q in range(3)]
-    h = pick(src[0, 7:8])
-
-    def near_step(k):
+    h = pick(src[hi, 7:8])
+
+    def own_step(k):
         tgt_copy(k).wait_recv()
-        near(k)
-
-    each(1, t, near_step)
-    each(1, s, lambda j: src_copy(j).wait_recv())
-
-    def far_step(k):
-        far(k, 1)
-        red_copy(k).start()
-
-    each(1, t, far_step)
-    far(0, 1)
+        add(k, hi, zeros, s == 1)
+
+    each(1, t, own_step)
+
+    for o in range(s - 1):
+        src_arrival(o).wait_recv()
+        if o < s - 2:
+            each(0, t, lambda k: add(k, nearest(o), [sums[k, q] for q in range(6)], False))
+
+    def last_step(i):
+        k = (n_ia // 2 + i % n_ia) % n_ia * n_lo + n_lo - 1 - i // n_ia
+        if s > 1:
+            add(k, nearest(s - 2), [sums[k, q] for q in range(6)], True)
+
+        @pl.when(k != 0)
+        def send():
+            red_copy(k).start()
+
+    each(0, t, last_step)
 
     def collect(k, total):
         red_copy(k).wait_recv()
@@ -188,7 +214,7 @@
         red_copy(k).wait_send()
 
     each(1, t, drain)
-    each(1, s, lambda j: src_copy(j).wait_send())
+    each(0, s - 1, lambda o: src_copy(o).wait_send())
 
 
 def on_device(shape, star_pos, star_vel, star_acc, star_jerk, star_mass, star_level,
@@ -200,7 +226,7 @@
     f32 = jnp.float32
     return pl.pallas_call(
         functools.partial(kernel, shape),
-        out_shape=jax.ShapeDtypeStruct((cap, 12), f32),
+        out_shape=pltpu.VMEM((cap, 12), f32),
         in_specs=[pl.BlockSpec(memory_space=pltpu.HBM)] * 8,
         out_specs=pl.BlockSpec(memory_space=pltpu.VMEM),
         scratch_shapes=[
@@ -217,6 +243,7 @@
             pltpu.SemaphoreType.DMA((s,)), pltpu.SemaphoreType.DMA((s,)),
             pltpu.SemaphoreType.DMA((t,)), pltpu.SemaphoreType.DMA((t,)),
             pltpu.SemaphoreType.DMA((t,)), pltpu.SemaphoreType.DMA((t,)),
+            pltpu.SemaphoreType.REGULAR,
         ],
         compiler_params=pltpu.CompilerParams(collective_id=0, has_side_effects=True),
     )(star_pos, star_vel, star_acc, star_jerk, star_mass.reshape(1, stars),

time: 19.4 us -> 16.4 us (0.85)
  Pallas kernels: 17.3 us -> 14.9 us
  local copies, waits for them, and re-layouts: 1.28 us -> 0.6 us
    pallas_call x1, Pallas kernels: 17.3 us -> 14.9 us  [on_device(): pl.pallas_call(functools.partial(kernel, shape), out_shape=pltpu.VMEM((ca...]
    unnamed x1, local copies, waits for them, and re-layouts: 1.28 us -> 0.6 us
where the time goes in v2:
time: 16.4 us; the launch traced here: 16.2 us
  Pallas kernels  14.9 us (91%)
  between operations  0.66 us (4%)
  local copies, waits for them, and re-layouts  0.6 us (4%)
    pallas_call x1, Pallas kernels, on_device(): pl.pallas_call(functools.partial(kernel, shape), out_shape=pltpu.VMEM((ca...  14.9 us
    unnamed x1, local copies, waits for them, and re-layouts  0.6 us

profile of v2, /device:TPU:0, one launch (start us, length us, event | category | flops | bytes accessed | tf_op | source)
XLA Modules:
  0.0 16.2 jit_solution(16300563388758684163)
XLA Ops:
  0.7 14.9 %shard_map.82 = f32[8,12]{1,0:T(8,128)S(1)} custom-call(f32[3,1024]{1,0:T(4,128)} %pos_hbm.1, f32[3,1024]{1,0:T(4,128)} %vel_hbm.1, f32[3,1024]{1,0:T(4,128)} %acc_hbm.1, f32[3,1024]{1,0:T(4,128)} %jerk_hbm.1, f32[1,1024]{1,0:T(1,128)} %bitcast.4, s32[1,1024]{1,0:T(1,128)} %bitcast.5, s32[8]{0:T(128)} %idx_hbm.1, s32[1]{0:T(128)S(6)} %copy.11.cnt_hbm), custom_call_target="tpu_custom_call" | custom-call | tf_op jit(solution)/shard_map/pallas_call | solution.py:227
  15.6 0.6 %copy.10 = f32[12,8]{0,1:T(8,128)} copy(f32[12,8]{0,1:T(8,128)S(1)} %bitcast.3) | data formatting | bytes 768

commit v3 on v2

--- a/solution.py
+++ b/solution.py
@@ -19,7 +19,7 @@
 
 def kernel(
     shape, pos_hbm, vel_hbm, acc_hbm, jerk_hbm, mass_hbm, level_hbm, idx_hbm, cnt_hbm, out_ref,
-    pos, vel, acc, jerk, mass, level, idx, cnt, src, tgt, sums, part, got,
+    pos, vel, acc, jerk, mass, level, idx, cnt, src, tgt, wide, sums, part, got,
     in_sem, src_send, src_recv, tgt_send, tgt_recv, red_send, red_recv, ready,
 ):
     n_ia, n_ja, s = shape
@@ -136,9 +136,7 @@
             pl.semaphore_wait(ready, 1)
             src_copy(2).start()
 
-    def pairs(k, j, totals):
-        tile = tgt[k]
-        target = [jnp.broadcast_to(tile[:, q:q + 1], (cap, LANES)) for q in range(6)]
+    def pairs(target, j, totals):
         totals = list(totals)
         for c in range(stars // LANES):
             row = [src[j, q:q + 1, c * LANES:(c + 1) * LANES] for q in range(7)]
@@ -155,39 +153,44 @@
 
     zeros = [jnp.zeros((cap, LANES), jnp.float32)] * 6
 
-    def add(k, place, totals, last):
-        totals = pairs(k, place, totals)
+    size = next(b for b in (4, 2, 1) if t % b == 0)
+
+    def add(i, place, first, last):
+        places = [i * size + b for b in range(size)]
+        ks = [(n_ia // 2 + p % n_ia) % n_ia * n_lo + n_lo - 1 - p // n_ia for p in places]
+        if first:
+            tiles = [tgt[k] for k in ks]
+            targets = [[jnp.broadcast_to(tile[:, q:q + 1], (cap, LANES)) for q in range(6)]
+                       for tile in tiles]
+            totals = [zeros] * size
+        else:
+            targets = [[wide[k, q] for q in range(6)] for k in ks]
+            totals = [[sums[k, q] for q in range(6)] for k in ks]
+        totals = [pairs(target, place, total) for target, total in zip(targets, totals)]
         if last:
-            part[k] = columns([jnp.sum(x, axis=1, keepdims=True) for x in totals])
-        else:
+            tiles = [columns([jnp.sum(x, axis=1, keepdims=True) for x in total])
+                     for total in totals]
+            for k, tile in zip(ks, tiles):
+                part[k] = tile
+            for k in ks:
+                @pl.when(k != 0)
+                def send(k=k):
+                    red_copy(k).start()
+            return
+        for k, target, total in zip(ks, targets, totals):
             for q in range(6):
-                sums[k, q] = totals[q]
-
-    add(0, hi, zeros, s == 1)
+                if first:
+                    wide[k, q] = target[q]
+                sums[k, q] = total[q]
+
     old = [pick(acc[q:q + 1, :]) for q in range(3)] + [pick(jerk[q:q + 1, :]) for q in range(3)]
     h = pick(src[hi, 7:8])
 
-    def own_step(k):
-        tgt_copy(k).wait_recv()
-        add(k, hi, zeros, s == 1)
-
-    each(1, t, own_step)
-
+    each(1, t, lambda k: tgt_copy(k).wait_recv())
+    each(0, t // size, lambda i: add(i, hi, True, s == 1))
     for o in range(s - 1):
         src_arrival(o).wait_recv()
-        if o < s - 2:
-            each(0, t, lambda k: add(k, nearest(o), [sums[k, q] for q in range(6)], False))
-
-    def last_step(i):
-        k = (n_ia // 2 + i % n_ia) % n_ia * n_lo + n_lo - 1 - i // n_ia
-        if s > 1:
-            add(k, nearest(s - 2), [sums[k, q] for q in range(6)], True)
-
-        @pl.when(k != 0)
-        def send():
-            red_copy(k).start()
-
-    each(0, t, last_step)
+        each(0, t // size, lambda i: add(i, nearest(o), False, o == s - 2))
 
     def collect(k, total):
         red_copy(k).wait_recv()
@@ -237,6 +240,7 @@
             pltpu.VMEM((s, 8, stars), f32),
             pltpu.VMEM((t, cap, LANES), f32),
             pltpu.VMEM((t, 6, cap, LANES), f32),
+            pltpu.VMEM((t, 6, cap, LANES), f32),
             pltpu.VMEM((t, cap, LANES), f32),
             pltpu.VMEM((t, cap, LANES), f32),
             pltpu.SemaphoreType.DMA((8,)),

time: 16.4 us -> 15.7 us (0.957)
  Pallas kernels: 14.9 us -> 14.3 us
    pallas_call x1, Pallas kernels: 14.9 us -> 14.3 us  [on_device(): pl.pallas_call(functools.partial(kernel, shape), out_shape=pltpu.VMEM((ca...]
where the time goes in v3:
time: 15.7 us; the launch traced here: 15.5 us
  Pallas kernels  14.3 us (91%)
  between operations  0.66 us (4%)
  local copies, waits for them, and re-layouts  0.6 us (4%)
    pallas_call x1, Pallas kernels, on_device(): pl.pallas_call(functools.partial(kernel, shape), out_shape=pltpu.VMEM((ca...  14.3 us
    unnamed x1, local copies, waits for them, and re-layouts  0.6 us

profile of v3, /device:TPU:0, one launch (start us, length us, event | category | flops | bytes accessed | tf_op | source)
XLA Modules:
  0.0 15.5 jit_solution(9300234357104344802)
XLA Ops:
  0.7 14.3 %shard_map.82 = f32[8,12]{1,0:T(8,128)S(1)} custom-call(f32[3,1024]{1,0:T(4,128)} %pos_hbm.1, f32[3,1024]{1,0:T(4,128)} %vel_hbm.1, f32[3,1024]{1,0:T(4,128)} %acc_hbm.1, f32[3,1024]{1,0:T(4,128)} %jerk_hbm.1, f32[1,1024]{1,0:T(1,128)} %bitcast.4, s32[1,1024]{1,0:T(1,128)} %bitcast.5, s32[8]{0:T(128)} %idx_hbm.1, s32[1]{0:T(128)S(6)} %copy.11.cnt_hbm), custom_call_target="tpu_custom_call" | custom-call | tf_op jit(solution)/shard_map/pallas_call | solution.py:230
  14.9 0.6 %copy.10 = f32[12,8]{0,1:T(8,128)} copy(f32[12,8]{0,1:T(8,128)S(1)} %bitcast.3) | data formatting | bytes 768
